TPU v7x, 512 devices: a whole 4x8x8 slice. The times are simulated.
512 devices in a mesh: member: 8 (over y_hi, x), lat: 64 (over y_lo, z, core).
Axes of the slice: x: 4, y: 8 (y_hi: 2, y_lo: 4; y = y_hi * 4 + y_lo), z: 8, core: 2. Of those that a mesh axis runs over, the one named last changes fastest.
Arguments:
- atmosphere: float32 [2, 16, 8, 384, 1536], P(None, 'member', None, 'lat'), may hold values from -4 to 4
- ocean_state: float32 [2, 384, 1536], P(None, 'lat', 'member'), may hold values from -4 to 4
- viscosity: float32 [384, 1536], P('lat', 'member'), may hold values from 0.02 to 0.2
- sea_mask: int32 [384, 1536], P('lat'), may hold values 0 or 1
- parameter_index: int32 [16], P('member'), may hold values from 0 to 31
- parameter_table: float32 [32, 3], replicated, may hold values from 0.1 to 0.3
- level_mix: float32 [8, 8], replicated, may hold values from -0.5 to 0.5
Outputs:
- atmos_out: float32 [2, 16, 8, 384, 1536], P(None, 'member', None, 'lat')
- ocean_out: float32 [2, 384, 1536], P(None, 'lat', 'member')
All inputs are finite; a program needn't handle non-finite values. No bound on the sum of `sea_mask` on one device may be relied on, other than what follows from the above.
Results may differ from a plain program's by a relative error of at most 0.00011.
Values sent between devices are 32-bit elements; how exact they have to be, the bound alone decides.
A program may use at most 64 MiB of HBM per device.

v0:
```python
import jax
import jax.numpy as jnp
from jax import lax
from jax.sharding import PartitionSpec as P

ASTEPS = 3
OSTEPS = 2
COUPLE = 2
ADVECTION = 0.1
OCEAN_GAIN = 0.5
OCEAN_DIFFUSION = 0.15


def with_halo(block, sides, width, periodic):
    for axis, dim in sides:
        count = lax.axis_size(axis)
        forward = [(i, i + 1) for i in range(count - 1)]
        if periodic:
            forward.append((count - 1, 0))
        backward = [(target, source) for source, target in forward]
        low = lax.ppermute(
            lax.slice_in_dim(block, block.shape[dim] - width, None, axis=dim), axis, forward
        )
        high = lax.ppermute(lax.slice_in_dim(block, 0, width, axis=dim), axis, backward)
        block = jnp.concatenate([low, block, high], axis=dim)
    return block


def lookup(parameter_index, parameter_table):
    onehot = (
        parameter_index[:, None] == jnp.arange(parameter_table.shape[0], dtype=jnp.int32)[None, :]
    ).astype(jnp.float32)
    picked = jnp.dot(
        onehot, parameter_table, precision=lax.Precision.HIGHEST, preferred_element_type=jnp.float32
    )
    return (0.6 * picked[:, 0], 2.0 * jnp.transpose(picked[:, 1:3]))


def atmos_step(padded_rows, surface, diffusivity, exchange, level_mix):
    centre = padded_rows[:, :, :, 1:-1, :]
    northern = padded_rows[:, :, :, 2:, :]
    southern = padded_rows[:, :, :, :-2, :]
    eastern = jnp.roll(centre, -1, axis=4)
    western = jnp.roll(centre, 1, axis=4)
    laplace = eastern + western + northern + southern - 4.0 * centre
    zonal_wind = centre[1]
    advected = (
        centre
        - ADVECTION * zonal_wind[None] * (eastern - western) * 0.5
        + diffusivity[None, :, None, None, None] * laplace
    )
    mixed_state = advected + jnp.einsum(
        "kl,fmlrn->fmkrn", level_mix, advected, precision=lax.Precision.HIGHEST
    )
    bottom = mixed_state[:, :, 0] + exchange[:, :, None, None] * (
        surface[:, None] - mixed_state[:, :, 0]
    )
    return mixed_state.at[:, :, 0].set(bottom)


def atmos_window(atmos_state, surface, diffusivity, exchange, level_mix):
    for substep in range(ASTEPS):
        padded_rows = with_halo(atmos_state, (("lat", 3),), 1, False)
        atmos_state = atmos_step(padded_rows, surface, diffusivity, exchange, level_mix)
    return atmos_state


def ocean_step(ocean, forcing, ocean_rate, ocean_mask):
    padded_ocean = with_halo(ocean, (("lat", 1),), 1, False)
    columns = with_halo(ocean, (("member", 2),), 1, True)
    eastern = columns[:, :, 2:]
    western = columns[:, :, :-2]
    laplace = padded_ocean[:, 2:] + padded_ocean[:, :-2] + eastern + western - 4.0 * ocean
    return ocean + ocean_mask[None] * (OCEAN_GAIN * forcing + ocean_rate * laplace)


def body(atmosphere, ocean_state, viscosity, sea_mask, parameter_index, parameter_table, level_mix):
    local_members = atmosphere.shape[1]
    tile_width = ocean_state.shape[2]
    members = local_members * lax.axis_size("member")
    diffusivity, exchange = lookup(parameter_index, parameter_table)
    full_mask = sea_mask.astype(jnp.float32)
    tile_start = lax.axis_index("member") * tile_width
    ocean = ocean_state
    ocean_mask = lax.dynamic_slice_in_dim(full_mask, tile_start, tile_width, 1)
    ocean_rate = jnp.stack([jnp.full_like(viscosity, OCEAN_DIFFUSION), viscosity])
    atmos_state = atmosphere
    for coupling in range(COUPLE):
        surface = lax.all_gather(ocean, "member", axis=2, tiled=True)
        atmos_state = atmos_window(atmos_state, surface, diffusivity, exchange, level_mix)
        flux_terms = jnp.sum(
            exchange[:, :, None, None] * (atmos_state[:, :, 0] - surface[:, None]), axis=1
        )
        forcing = lax.psum_scatter(flux_terms, "member", scatter_dimension=2, tiled=True) / members
        for substep in range(OSTEPS):
            ocean = ocean_step(ocean, forcing, ocean_rate, ocean_mask)
    return (atmos_state, ocean)


def solution(mesh):
    return jax.shard_map(
        body,
        mesh=mesh,
        in_specs=(
            P(None, "member", None, "lat", None),
            P(None, "lat", "member"),
            P("lat", "member"),
            P("lat", None),
            P("member"),
            P(),
            P(),
        ),
        out_specs=(P(None, "member", None, "lat", None), P(None, "lat", "member")),
        check_vma=False,
    )
```

profile of v0, /device:TPU:48, one launch (start us, length us, event | category | flops | bytes accessed | tf_op | source)
XLA Modules:
  0.0 473.0 jit_solution(4835626749836713685)
XLA Ops:
  8.3 11.2 %collective-permute-start = (f32[2,2,8,1,1536]{4,2,3,1,0:T(8,128)S(1)}, f32[2,2,8,1,1536]{4,2,3,1,0:T(8,128)}, u32[]{:S(2)}, u32[]{:S(2)}) collective-permute-start(f32[2,2,8,1,1536]{4,2,3,1,0:T(8,128)S(1)} %get-tuple-element.118), channel_id=1, source_target_pairs={{1,0},{2,1},{3,2},{4,3},{5,4},{6,5},{7,6},{8,7},{9,8},{10,9},{11,1... | collective-permute-start | bytes 589832 | tf_op jit(solution)/shard_map/ppermute | solution.py:24
  19.5 1.9 collective-permute-start.1
  22.8 5.1 %collective-permute-start.10 = (f32[2,6,1]{2,1,0:T(8,128)}, f32[2,6,1]{2,1,0:T(8,128)}, u32[]{:S(2)}, u32[]{:S(2)}) collective-permute-start(f32[2,6,1]{2,1,0:T(8,128)} %get-tuple-element.132), channel_id=1, source_target_pairs={{64,0},{128,64},{192,128},{256,192},{320,256},{384,320},{448,384},... | collective-permute-start | bytes 152 | tf_op jit(solution)/shard_map/ppermute | solution.py:24
  27.9 1.9 collective-permute-start.11
  31.1 5.6 %collective-permute-start.8 = (f32[2,1,192]{2,1,0:T(1,128)}, f32[2,1,192]{2,1,0:T(1,128)}, u32[]{:S(2)}, u32[]{:S(2)}) collective-permute-start(f32[2,1,192]{2,1,0:T(1,128)} %copy.68), channel_id=1, source_target_pairs={{1,0},{2,1},{3,2},{4,3},{5,4},{6,5},{7,6},{8,7},{9,8},{10,9},{11,1... | collective-permute-start | bytes 4616 | tf_op jit(solution)/shard_map/ppermute | solution.py:24
  36.7 3.5 fusion.206
  42.3 50.8 %all_gather.6 = f32[2,6,1536]{1,0,2:T(2,128)S(1)} all-gather(f32[2,6,192]{1,0,2:T(2,128)S(1)} %copy.63), channel_id=1, replica_groups=mesh['member'=8,'lat'=64] {'member'}, dimensions={2}, use_global_device_ids=true | all-gather | bytes 82944 | tf_op jit(solution)/shard_map/all_gather | solution.py:89
  96.3 5.4 %fusion.5 = f32[2,2,8,6,1536]{4,2,3,1,0:T(8,128)S(1)} fusion(f32[2,2,8,6,1536]{4,2,3,1,0:T(8,128)S(1)} %copy-done.1, f32[2,2,8,1,1536]{4,2,3,1,0:T(8,128)} %collective-permute-done.1, f32[2,2,8,1,1536]{4,2,3,1,0:T(8,128)} %collective-permute-done, f32[2,2,8,6,1535]{4,2,3,1,0:T(8,128)} %get-tuple-element.115, f32[2,2,8,6,1]{4,2,3,1,0:T(8,128)S(1)} %get-tuple-element.117, ...), kind=kOutput, calls=%fused_computation.11 | convolution fusion | flops 37453824 | bytes 5701896 | tf_op jit(solution)/shard_map/kl,fmlrn->fmkrn/dot_general | solution.py:52
  103.4 1.9 collective-permute-start.2
  105.3 2.4 collective-permute-start.3
  108.5 5.9 %collective-permute-done.3 = f32[2,2,8,1,1536]{4,2,3,1,0:T(8,128)S(1)} collective-permute-done((f32[2,2,8,1,1536]{4,2,3,1,0:T(8,128)S(1)}, f32[2,2,8,1,1536]{4,2,3,1,0:T(8,128)S(1)}, u32[]{:S(2)}, u32[]{:S(2)}) %collective-permute-start.3) | collective-permute-done | bytes 196640 | tf_op jit(solution)/shard_map/ppermute | solution.py:21
  114.4 2.6 fusion.4
  118.8 1.9 collective-permute-start.4
  120.7 2.4 collective-permute-start.5
  123.9 1.9 collective-permute-start.9
  125.8 4.0 collective-permute-done.5
  129.8 2.6 fusion.3
  133.7 1.8 fusion.197
  138.3 1.8 reshape.255
  140.9 1.9 collective-permute-start.6
  142.8 82.0 %reduce-scatter.7.cloned.1.call-done = f32[192,12]{1,0:T(8,128)} async-done(((f32[1536,12]{1,0:T(8,128)}), f32[192,12]{1,0:T(8,128)}) %reduce-scatter.7.cloned.1.call-update) | async-done | bytes 9232
  226.0 1.9 collective-permute-start.7
  228.8 5.8 %collective-permute-start.12 = (f32[2,1,192]{2,1,0:T(1,128)S(1)}, f32[2,1,192]{2,1,0:T(1,128)S(1)}, u32[]{:S(2)}, u32[]{:S(2)}) collective-permute-start(f32[2,1,192]{2,1,0:T(1,128)S(1)} %get-tuple-element.128), channel_id=1, source_target_pairs={{1,0},{2,1},{3,2},{4,3},{5,4},{6,5},{7,6},{8,7},{9,8},{10,9},{11,1... | collective-permute-start | bytes 4616 | tf_op jit(solution)/shard_map/ppermute | solution.py:24
  234.6 1.9 collective-permute-start.13
  236.6 6.6 %collective-permute-start.14 = (f32[2,6,1]{2,1,0:T(8,128)S(1)}, f32[2,6,1]{2,1,0:T(8,128)S(1)}, u32[]{:S(2)}, u32[]{:S(2)}) collective-permute-start(f32[2,6,1]{2,1,0:T(8,128)S(1)} %get-tuple-element.130), channel_id=1, source_target_pairs={{64,0},{128,64},{192,128},{256,192},{320,256},{384,320},{448,384},... | collective-permute-start | bytes 152 | tf_op jit(solution)/shard_map/ppermute | solution.py:24
  244.5 2.1 collective-permute-start.15
  246.6 9.9 %collective-permute-done.15 = f32[2,6,1]{2,1,0:T(8,128)S(1)} collective-permute-done((f32[2,6,1]{2,1,0:T(8,128)S(1)}, f32[2,6,1]{2,1,0:T(8,128)S(1)}, u32[]{:S(2)}, u32[]{:S(2)}) %collective-permute-start.15) | collective-permute-done | bytes 80 | tf_op jit(solution)/shard_map/ppermute | solution.py:21
  256.8 51.3 %all_gather.7 = f32[2,6,1536]{1,0,2:T(2,128)S(1)} all-gather(f32[2,6,192]{1,0,2:T(2,128)S(1)} %copy.78), channel_id=1, replica_groups=mesh['member'=8,'lat'=64] {'member'}, dimensions={2}, use_global_device_ids=true | all-gather | bytes 82944 | tf_op jit(solution)/shard_map/all_gather | solution.py:89
  308.8 1.9 collective-permute-start.20
  310.8 2.4 collective-permute-start.21
  313.2 5.2 %fusion.2 = f32[2,2,8,6,1536]{4,2,3,1,0:T(8,128)S(1)} fusion(f32[2,2,8,6,1536]{4,2,3,1,0:T(8,128)S(1)} %scatter.24, f32[2,2,8,1,1536]{4,2,3,1,0:T(8,128)} %collective-permute-done.7, f32[2,2,8,1,1536]{4,2,3,1,0:T(8,128)} %collective-permute-done.6, f32[2,2,8,6,1535]{4,2,3,1,0:T(8,128)} %get-tuple-element.97, f32[2,2,8,6,1]{4,2,3,1,0:T(8,128)} %get-tuple-element.99, ...), kind=kOutput, calls=%fused_computation.5 | convolution fusion | flops 37453824 | bytes 5701896 | tf_op jit(solution)/shard_map/kl,fmlrn->fmkrn/dot_general | solution.py:52
  320.1 5.3 %collective-permute-start.16 = (f32[2,2,8,1,1536]{4,2,3,1,0:T(8,128)S(1)}, f32[2,2,8,1,1536]{4,2,3,1,0:T(8,128)S(1)}, u32[]{:S(2)}, u32[]{:S(2)}) collective-permute-start(f32[2,2,8,1,1536]{4,2,3,1,0:T(8,128)S(1)} %get-tuple-element.92), channel_id=1, source_target_pairs={{1,0},{2,1},{3,2},{4,3},{5,4},{6,5},{7,6},{8,7},{9,8},{10,9},{11,1... | collective-permute-start | bytes 589832 | tf_op jit(solution)/shard_map/ppermute | solution.py:24
  325.4 1.9 collective-permute-start.17
  328.5 5.9 %collective-permute-done.17 = f32[2,2,8,1,1536]{4,2,3,1,0:T(8,128)S(1)} collective-permute-done((f32[2,2,8,1,1536]{4,2,3,1,0:T(8,128)S(1)}, f32[2,2,8,1,1536]{4,2,3,1,0:T(8,128)S(1)}, u32[]{:S(2)}, u32[]{:S(2)}) %collective-permute-start.17) | collective-permute-done | bytes 196640 | tf_op jit(solution)/shard_map/ppermute | solution.py:21
  334.5 2.6 fusion.1
  338.8 1.9 collective-permute-start.18
  340.7 2.4 collective-permute-start.19
  343.9 5.9 %collective-permute-done.19 = f32[2,2,8,1,1536]{4,2,3,1,0:T(8,128)S(1)} collective-permute-done((f32[2,2,8,1,1536]{4,2,3,1,0:T(8,128)S(1)}, f32[2,2,8,1,1536]{4,2,3,1,0:T(8,128)S(1)}, u32[]{:S(2)}, u32[]{:S(2)}) %collective-permute-start.19) | collective-permute-done | bytes 196640 | tf_op jit(solution)/shard_map/ppermute | solution.py:21
  349.8 2.6 fusion
  354.0 1.8 reshape.257
  355.9 1.9 collective-permute-start.22
  357.8 3.9 collective-permute-start.23
  362.6 76.5 %reduce-scatter.9.cloned.1.call-done = f32[192,12]{1,0:T(8,128)} async-done(((f32[1536,12]{1,0:T(8,128)}), f32[192,12]{1,0:T(8,128)}) %reduce-scatter.9.cloned.1.call-update) | async-done | bytes 9232
  440.4 3.5 collective-permute-start.24
  443.9 1.9 collective-permute-start.25
  445.9 8.0 %collective-permute-start.26 = (f32[2,6,1]{2,1,0:T(8,128)S(1)}, f32[2,6,1]{2,1,0:T(8,128)S(1)}, u32[]{:S(2)}, u32[]{:S(2)}) collective-permute-start(f32[2,6,1]{2,1,0:T(8,128)S(1)} %get-tuple-element.122), channel_id=1, source_target_pairs={{64,0},{128,64},{192,128},{256,192},{320,256},{384,320},{448,384},... | collective-permute-start | bytes 152 | tf_op jit(solution)/shard_map/ppermute | solution.py:24
  453.9 1.9 collective-permute-start.27
  455.9 9.6 %collective-permute-done.27 = f32[2,6,1]{2,1,0:T(8,128)S(1)} collective-permute-done((f32[2,6,1]{2,1,0:T(8,128)S(1)}, f32[2,6,1]{2,1,0:T(8,128)S(1)}, u32[]{:S(2)}, u32[]{:S(2)}) %collective-permute-start.27) | collective-permute-done | bytes 80 | tf_op jit(solution)/shard_map/ppermute | solution.py:21
  (127 shorter events, 33.1 us)
Async XLA Ops:
  7.2 89.1 %copy-start = (f32[8,8]{1,0:T(8,128)S(1)}, f32[8,8]{1,0:T(8,128)}, u32[]{:S(2)}) copy-start(f32[8,8]{1,0:T(8,128)} %param.25) | copy-start | bytes 772
  7.2 217.7 %reduce-scatter.7.cloned.1.call-start = ((), (), s32[]{:S(2)}) async-start(), calls=%async_computation.2 | async-start | bytes 884736
  8.3 87.9 %collective-permute-start = (f32[2,2,8,1,1536]{4,2,3,1,0:T(8,128)S(1)}, f32[2,2,8,1,1536]{4,2,3,1,0:T(8,128)}, u32[]{:S(2)}, u32[]{:S(2)}) collective-permute-start(f32[2,2,8,1,1536]{4,2,3,1,0:T(8,128)S(1)} %get-tuple-element.118), channel_id=1, source_target_pairs={{1,0},{2,1},{3,2},{4,3},{5,4},{6,5},{7,6},{8,7},{9,8},{10,9},{11,1... | collective-permute-start | bytes 589832 | tf_op jit(solution)/shard_map/ppermute | solution.py:24
  19.5 76.8 %collective-permute-start.1 = (f32[2,2,8,1,1536]{4,2,3,1,0:T(8,128)S(1)}, f32[2,2,8,1,1536]{4,2,3,1,0:T(8,128)}, u32[]{:S(2)}, u32[]{:S(2)}) collective-permute-start(f32[2,2,8,1,1536]{4,2,3,1,0:T(8,128)S(1)} %get-tuple-element.119), channel_id=1, source_target_pairs={{0,1},{1,2},{2,3},{3,4},{4,5},{5,6},{6,7},{7,8},{8,9},{9,10},{10,1... | collective-permute-start | bytes 589832 | tf_op jit(solution)/shard_map/ppermute | solution.py:21
  22.1 8.4 %copy-start.6 = (f32[2,6,192]{2,1,0:T(8,128)}, f32[2,6,192]{2,1,0:T(8,128)S(1)}, u32[]{:S(2)}) copy-start(f32[2,6,192]{2,1,0:T(8,128)S(1)} %copy.77) | copy-start | bytes 27652
  22.8 203.2 %collective-permute-start.10 = (f32[2,6,1]{2,1,0:T(8,128)}, f32[2,6,1]{2,1,0:T(8,128)}, u32[]{:S(2)}, u32[]{:S(2)}) collective-permute-start(f32[2,6,1]{2,1,0:T(8,128)} %get-tuple-element.132), channel_id=1, source_target_pairs={{64,0},{128,64},{192,128},{256,192},{320,256},{384,320},{448,384},... | collective-permute-start | bytes 152 | tf_op jit(solution)/shard_map/ppermute | solution.py:24
  27.9 200.1 %collective-permute-start.11 = (f32[2,6,1]{2,1,0:T(8,128)}, f32[2,6,1]{2,1,0:T(8,128)}, u32[]{:S(2)}, u32[]{:S(2)}) collective-permute-start(f32[2,6,1]{2,1,0:T(8,128)} %get-tuple-element.133), channel_id=1, source_target_pairs={{0,64},{64,128},{128,192},{192,256},{256,320},{320,384},{384,448},... | collective-permute-start | bytes 152 | tf_op jit(solution)/shard_map/ppermute | solution.py:21
  31.1 9.1 %copy-start.1 = (f32[2,2,8,6,1536]{4,2,3,1,0:T(8,128)S(1)}, f32[2,2,8,6,1536]{4,2,3,1,0:T(8,128)}, u32[]{:S(2)}) copy-start(f32[2,2,8,6,1536]{4,2,3,1,0:T(8,128)} %param.19) | copy-start | bytes 3538948
  31.1 10.0 %copy-start.12 = (f32[32,3]{0,1:T(4,128)S(1)}, f32[32,3]{0,1:T(4,128)}, u32[]{:S(2)}) copy-start(f32[32,3]{0,1:T(4,128)} %param.24) | copy-start | bytes 1156
  31.1 10.0 %copy-start.13 = (s32[2]{0:T(128)S(1)}, s32[2]{0:T(128)}, u32[]{:S(2)}) copy-start(s32[2]{0:T(128)} %param.23) | copy-start | bytes 28
  31.1 196.8 %collective-permute-start.8 = (f32[2,1,192]{2,1,0:T(1,128)}, f32[2,1,192]{2,1,0:T(1,128)}, u32[]{:S(2)}, u32[]{:S(2)}) collective-permute-start(f32[2,1,192]{2,1,0:T(1,128)} %copy.68), channel_id=1, source_target_pairs={{1,0},{2,1},{3,2},{4,3},{5,4},{6,5},{7,6},{8,7},{9,8},{10,9},{11,1... | collective-permute-start | bytes 4616 | tf_op jit(solution)/shard_map/ppermute | solution.py:24
  40.2 1.9 copy-start.9
  96.3 5.4 %copy-start.2 = (f32[2,6,1536]{2,1,0:T(8,128)S(1)}, f32[2,6,1536]{2,1,0:T(8,128)}, u32[]{:S(2)}) copy-start(f32[2,6,1536]{2,1,0:T(8,128)} %copy.64) | copy-start | bytes 221188
  103.3 11.1 %copy-start.14 = (f32[2]{0:T(128)S(1)}, f32[2]{0:T(128)}, u32[]{:S(2)}) copy-start(f32[2]{0:T(128)} %multiply_reduce_fusion) | copy-start | bytes 28
  103.4 5.1 %collective-permute-start.2 = (f32[2,2,8,1,1536]{4,2,3,1,0:T(8,128)S(1)}, f32[2,2,8,1,1536]{4,2,3,1,0:T(8,128)S(1)}, u32[]{:S(2)}, u32[]{:S(2)}) collective-permute-start(f32[2,2,8,1,1536]{4,2,3,1,0:T(8,128)S(1)} %get-tuple-element.112), channel_id=1, source_target_pairs={{1,0},{2,1},{3,2},{4,3},{5,4},{6,5},{7,6},{8,7},{9,8},{10,9},{11,1... | collective-permute-start | bytes 589832 | tf_op jit(solution)/shard_map/ppermute | solution.py:24
  105.3 9.1 %collective-permute-start.3 = (f32[2,2,8,1,1536]{4,2,3,1,0:T(8,128)S(1)}, f32[2,2,8,1,1536]{4,2,3,1,0:T(8,128)S(1)}, u32[]{:S(2)}, u32[]{:S(2)}) collective-permute-start(f32[2,2,8,1,1536]{4,2,3,1,0:T(8,128)S(1)} %get-tuple-element.113), channel_id=1, source_target_pairs={{0,1},{1,2},{2,3},{3,4},{4,5},{5,6},{6,7},{7,8},{8,9},{9,10},{10,1... | collective-permute-start | bytes 589832 | tf_op jit(solution)/shard_map/ppermute | solution.py:21
  114.4 2.6 copy-start.3
  118.7 5.2 %copy-start.11 = (f32[2,1,192]{2,1,0:T(1,128)S(1)}, f32[2,1,192]{2,1,0:T(1,128)}, u32[]{:S(2)}) copy-start(f32[2,1,192]{2,1,0:T(1,128)} %copy.70) | copy-start | bytes 4612
  118.7 11.1 %copy-start.15 = (f32[2]{0:T(128)S(1)}, f32[2]{0:T(128)}, u32[]{:S(2)}) copy-start(f32[2]{0:T(128)} %multiply_reduce_fusion) | copy-start | bytes 28
  118.8 5.1 %collective-permute-start.4 = (f32[2,2,8,1,1536]{4,2,3,1,0:T(8,128)S(1)}, f32[2,2,8,1,1536]{4,2,3,1,0:T(8,128)S(1)}, u32[]{:S(2)}, u32[]{:S(2)}) collective-permute-start(f32[2,2,8,1,1536]{4,2,3,1,0:T(8,128)S(1)} %get-tuple-element.106), channel_id=1, source_target_pairs={{1,0},{2,1},{3,2},{4,3},{5,4},{6,5},{7,6},{8,7},{9,8},{10,9},{11,1... | collective-permute-start | bytes 589832 | tf_op jit(solution)/shard_map/ppermute | solution.py:24
  120.7 9.1 %collective-permute-start.5 = (f32[2,2,8,1,1536]{4,2,3,1,0:T(8,128)S(1)}, f32[2,2,8,1,1536]{4,2,3,1,0:T(8,128)S(1)}, u32[]{:S(2)}, u32[]{:S(2)}) collective-permute-start(f32[2,2,8,1,1536]{4,2,3,1,0:T(8,128)S(1)} %get-tuple-element.107), channel_id=1, source_target_pairs={{0,1},{1,2},{2,3},{3,4},{4,5},{5,6},{6,7},{7,8},{8,9},{9,10},{10,1... | collective-permute-start | bytes 589832 | tf_op jit(solution)/shard_map/ppermute | solution.py:21
  123.9 104.1 %collective-permute-start.9 = (f32[2,1,192]{2,1,0:T(1,128)S(1)}, f32[2,1,192]{2,1,0:T(1,128)S(1)}, u32[]{:S(2)}, u32[]{:S(2)}) collective-permute-start(f32[2,1,192]{2,1,0:T(1,128)S(1)} %copy-done.11), channel_id=1, source_target_pairs={{0,1},{1,2},{2,3},{3,4},{4,5},{5,6},{6,7},{7,8},{8,9},{9,10},{10,1... | collective-permute-start | bytes 4616 | tf_op jit(solution)/shard_map/ppermute | solution.py:21
  129.8 2.6 copy-start.4
  140.1 87.9 %copy-start.7 = (f32[2,6,192]{2,1,0:T(8,128)S(1)}, f32[2,6,192]{2,1,0:T(8,128)}, u32[]{:S(2)}) copy-start(f32[2,6,192]{2,1,0:T(8,128)} %copy-done.6) | copy-start | bytes 27652
  140.1 87.9 %copy-start.8 = (f32[6,192]{1,0:T(8,128)S(1)}, f32[6,192]{1,0:T(8,128)}, u32[]{:S(2)}) copy-start(f32[6,192]{1,0:T(8,128)} %param.21) | copy-start | bytes 13828
  140.1 299.0 %reduce-scatter.9.cloned.1.call-start = ((), (), s32[]{:S(2)}) async-start(), calls=%async_computation.3 | async-start | bytes 884736
  140.9 172.3 %collective-permute-start.6 = (f32[2,2,8,1,1536]{4,2,3,1,0:T(8,128)}, f32[2,2,8,1,1536]{4,2,3,1,0:T(8,128)}, u32[]{:S(2)}, u32[]{:S(2)}) collective-permute-start(f32[2,2,8,1,1536]{4,2,3,1,0:T(8,128)} %get-tuple-element.100), channel_id=1, source_target_pairs={{1,0},{2,1},{3,2},{4,3},{5,4},{6,5},{7,6},{8,7},{9,8},{10,9},{11,1... | collective-permute-start | bytes 589832 | tf_op jit(solution)/shard_map/ppermute | solution.py:24
  226.0 87.2 %collective-permute-start.7 = (f32[2,2,8,1,1536]{4,2,3,1,0:T(8,128)}, f32[2,2,8,1,1536]{4,2,3,1,0:T(8,128)}, u32[]{:S(2)}, u32[]{:S(2)}) collective-permute-start(f32[2,2,8,1,1536]{4,2,3,1,0:T(8,128)} %get-tuple-element.101), channel_id=1, source_target_pairs={{0,1},{1,2},{2,3},{3,4},{4,5},{5,6},{6,7},{7,8},{8,9},{9,10},{10,1... | collective-permute-start | bytes 589832 | tf_op jit(solution)/shard_map/ppermute | solution.py:21
  228.8 27.7 %collective-permute-start.12 = (f32[2,1,192]{2,1,0:T(1,128)S(1)}, f32[2,1,192]{2,1,0:T(1,128)S(1)}, u32[]{:S(2)}, u32[]{:S(2)}) collective-permute-start(f32[2,1,192]{2,1,0:T(1,128)S(1)} %get-tuple-element.128), channel_id=1, source_target_pairs={{1,0},{2,1},{3,2},{4,3},{5,4},{6,5},{7,6},{8,7},{9,8},{10,9},{11,1... | collective-permute-start | bytes 4616 | tf_op jit(solution)/shard_map/ppermute | solution.py:24
  234.6 21.9 %collective-permute-start.13 = (f32[2,1,192]{2,1,0:T(1,128)S(1)}, f32[2,1,192]{2,1,0:T(1,128)S(1)}, u32[]{:S(2)}, u32[]{:S(2)}) collective-permute-start(f32[2,1,192]{2,1,0:T(1,128)S(1)} %get-tuple-element.129), channel_id=1, source_target_pairs={{0,1},{1,2},{2,3},{3,4},{4,5},{5,6},{6,7},{7,8},{8,9},{9,10},{10,1... | collective-permute-start | bytes 4616 | tf_op jit(solution)/shard_map/ppermute | solution.py:21
  236.6 7.9 %collective-permute-start.14 = (f32[2,6,1]{2,1,0:T(8,128)S(1)}, f32[2,6,1]{2,1,0:T(8,128)S(1)}, u32[]{:S(2)}, u32[]{:S(2)}) collective-permute-start(f32[2,6,1]{2,1,0:T(8,128)S(1)} %get-tuple-element.130), channel_id=1, source_target_pairs={{64,0},{128,64},{192,128},{256,192},{320,256},{384,320},{448,384},... | collective-permute-start | bytes 152 | tf_op jit(solution)/shard_map/ppermute | solution.py:24
  244.5 12.0 %collective-permute-start.15 = (f32[2,6,1]{2,1,0:T(8,128)S(1)}, f32[2,6,1]{2,1,0:T(8,128)S(1)}, u32[]{:S(2)}, u32[]{:S(2)}) collective-permute-start(f32[2,6,1]{2,1,0:T(8,128)S(1)} %get-tuple-element.131), channel_id=1, source_target_pairs={{0,64},{64,128},{128,192},{192,256},{256,320},{320,384},{384,448},... | collective-permute-start | bytes 152 | tf_op jit(solution)/shard_map/ppermute | solution.py:21
  308.1 5.1 %copy-start.5 = (f32[2,8,6,1536]{3,1,2,0:T(8,128)S(1)}, f32[2,8,6,1536]{3,1,2,0:T(8,128)}, u32[]{:S(2)}) copy-start(f32[2,8,6,1536]{3,1,2,0:T(8,128)} %fusion.98) | copy-start | bytes 1769476
  308.1 5.1 %copy-start.16 = (f32[2]{0:T(128)S(1)}, f32[2]{0:T(128)}, u32[]{:S(2)}) copy-start(f32[2]{0:T(128)} %multiply_reduce_fusion) | copy-start | bytes 28
  308.8 131.5 %collective-permute-start.20 = (f32[2,1,192]{2,1,0:T(1,128)S(1)}, f32[2,1,192]{2,1,0:T(1,128)S(1)}, u32[]{:S(2)}, u32[]{:S(2)}) collective-permute-start(f32[2,1,192]{2,1,0:T(1,128)S(1)} %get-tuple-element.124), channel_id=1, source_target_pairs={{1,0},{2,1},{3,2},{4,3},{5,4},{6,5},{7,6},{8,7},{9,8},{10,9},{11,1... | collective-permute-start | bytes 4616 | tf_op jit(solution)/shard_map/ppermute | solution.py:24
  310.8 129.6 %collective-permute-start.21 = (f32[2,1,192]{2,1,0:T(1,128)S(1)}, f32[2,1,192]{2,1,0:T(1,128)S(1)}, u32[]{:S(2)}, u32[]{:S(2)}) collective-permute-start(f32[2,1,192]{2,1,0:T(1,128)S(1)} %get-tuple-element.125), channel_id=1, source_target_pairs={{0,1},{1,2},{2,3},{3,4},{4,5},{5,6},{6,7},{7,8},{8,9},{9,10},{10,1... | collective-permute-start | bytes 4616 | tf_op jit(solution)/shard_map/ppermute | solution.py:21
  320.1 8.4 %collective-permute-start.16 = (f32[2,2,8,1,1536]{4,2,3,1,0:T(8,128)S(1)}, f32[2,2,8,1,1536]{4,2,3,1,0:T(8,128)S(1)}, u32[]{:S(2)}, u32[]{:S(2)}) collective-permute-start(f32[2,2,8,1,1536]{4,2,3,1,0:T(8,128)S(1)} %get-tuple-element.92), channel_id=1, source_target_pairs={{1,0},{2,1},{3,2},{4,3},{5,4},{6,5},{7,6},{8,7},{9,8},{10,9},{11,1... | collective-permute-start | bytes 589832 | tf_op jit(solution)/shard_map/ppermute | solution.py:24
  325.4 9.1 %collective-permute-start.17 = (f32[2,2,8,1,1536]{4,2,3,1,0:T(8,128)S(1)}, f32[2,2,8,1,1536]{4,2,3,1,0:T(8,128)S(1)}, u32[]{:S(2)}, u32[]{:S(2)}) collective-permute-start(f32[2,2,8,1,1536]{4,2,3,1,0:T(8,128)S(1)} %get-tuple-element.93), channel_id=1, source_target_pairs={{0,1},{1,2},{2,3},{3,4},{4,5},{5,6},{6,7},{7,8},{8,9},{9,10},{10,1... | collective-permute-start | bytes 589832 | tf_op jit(solution)/shard_map/ppermute | solution.py:21
  338.8 5.1 %collective-permute-start.18 = (f32[2,2,8,1,1536]{4,2,3,1,0:T(8,128)S(1)}, f32[2,2,8,1,1536]{4,2,3,1,0:T(8,128)S(1)}, u32[]{:S(2)}, u32[]{:S(2)}) collective-permute-start(f32[2,2,8,1,1536]{4,2,3,1,0:T(8,128)S(1)} %get-tuple-element.86), channel_id=1, source_target_pairs={{1,0},{2,1},{3,2},{4,3},{5,4},{6,5},{7,6},{8,7},{9,8},{10,9},{11,1... | collective-permute-start | bytes 589832 | tf_op jit(solution)/shard_map/ppermute | solution.py:24
  340.7 9.1 %collective-permute-start.19 = (f32[2,2,8,1,1536]{4,2,3,1,0:T(8,128)S(1)}, f32[2,2,8,1,1536]{4,2,3,1,0:T(8,128)S(1)}, u32[]{:S(2)}, u32[]{:S(2)}) collective-permute-start(f32[2,2,8,1,1536]{4,2,3,1,0:T(8,128)S(1)} %get-tuple-element.87), channel_id=1, source_target_pairs={{0,1},{1,2},{2,3},{3,4},{4,5},{5,6},{6,7},{7,8},{8,9},{9,10},{10,1... | collective-permute-start | bytes 589832 | tf_op jit(solution)/shard_map/ppermute | solution.py:21
  355.9 84.4 %collective-permute-start.22 = (f32[2,6,1]{2,1,0:T(8,128)S(1)}, f32[2,6,1]{2,1,0:T(8,128)S(1)}, u32[]{:S(2)}, u32[]{:S(2)}) collective-permute-start(f32[2,6,1]{2,1,0:T(8,128)S(1)} %get-tuple-element.126), channel_id=1, source_target_pairs={{64,0},{128,64},{192,128},{256,192},{320,256},{384,320},{448,384},... | collective-permute-start | bytes 152 | tf_op jit(solution)/shard_map/ppermute | solution.py:24
  357.8 82.5 %collective-permute-start.23 = (f32[2,6,1]{2,1,0:T(8,128)S(1)}, f32[2,6,1]{2,1,0:T(8,128)S(1)}, u32[]{:S(2)}, u32[]{:S(2)}) collective-permute-start(f32[2,6,1]{2,1,0:T(8,128)S(1)} %get-tuple-element.127), channel_id=1, source_target_pairs={{0,64},{64,128},{128,192},{192,256},{256,320},{320,384},{384,448},... | collective-permute-start | bytes 152 | tf_op jit(solution)/shard_map/ppermute | solution.py:21
  362.6 103.6 %copy-start.10 = (f32[2,2,8,6,1536]{4,2,3,1,0:T(8,128)}, f32[2,2,8,6,1536]{4,2,3,1,0:T(8,128)S(1)}, u32[]{:S(2)}) copy-start(f32[2,2,8,6,1536]{4,2,3,1,0:T(8,128)S(1)} %scatter.29) | copy-start | bytes 3538948
  440.4 25.0 %collective-permute-start.24 = (f32[2,1,192]{2,1,0:T(1,128)S(1)}, f32[2,1,192]{2,1,0:T(1,128)S(1)}, u32[]{:S(2)}, u32[]{:S(2)}) collective-permute-start(f32[2,1,192]{2,1,0:T(1,128)S(1)} %get-tuple-element.120), channel_id=1, source_target_pairs={{1,0},{2,1},{3,2},{4,3},{5,4},{6,5},{7,6},{8,7},{9,8},{10,9},{11,1... | collective-permute-start | bytes 4616 | tf_op jit(solution)/shard_map/ppermute | solution.py:24
  443.9 21.6 %collective-permute-start.25 = (f32[2,1,192]{2,1,0:T(1,128)S(1)}, f32[2,1,192]{2,1,0:T(1,128)S(1)}, u32[]{:S(2)}, u32[]{:S(2)}) collective-permute-start(f32[2,1,192]{2,1,0:T(1,128)S(1)} %get-tuple-element.121), channel_id=1, source_target_pairs={{0,1},{1,2},{2,3},{3,4},{4,5},{5,6},{6,7},{7,8},{8,9},{9,10},{10,1... | collective-permute-start | bytes 4616 | tf_op jit(solution)/shard_map/ppermute | solution.py:21
  445.9 9.9 %collective-permute-start.26 = (f32[2,6,1]{2,1,0:T(8,128)S(1)}, f32[2,6,1]{2,1,0:T(8,128)S(1)}, u32[]{:S(2)}, u32[]{:S(2)}) collective-permute-start(f32[2,6,1]{2,1,0:T(8,128)S(1)} %get-tuple-element.122), channel_id=1, source_target_pairs={{64,0},{128,64},{192,128},{256,192},{320,256},{384,320},{448,384},... | collective-permute-start | bytes 152 | tf_op jit(solution)/shard_map/ppermute | solution.py:24
  453.9 11.6 %collective-permute-start.27 = (f32[2,6,1]{2,1,0:T(8,128)S(1)}, f32[2,6,1]{2,1,0:T(8,128)S(1)}, u32[]{:S(2)}, u32[]{:S(2)}) collective-permute-start(f32[2,6,1]{2,1,0:T(8,128)S(1)} %get-tuple-element.123), channel_id=1, source_target_pairs={{0,64},{64,128},{128,192},{192,256},{256,320},{320,384},{384,448},... | collective-permute-start | bytes 152 | tf_op jit(solution)/shard_map/ppermute | solution.py:21
Sparse Core Ops, SparseCore 0:
  140.2 84.5 reduce-scatter.6
  355.9 83.1 reduce-scatter.8
where the time goes:
time: 474 us; the launch traced here: 473 us
  waiting for transfers between devices  204 us (43%)
  blocking collectives  102 us (22%)
  starting transfers between devices  93.5 us (20%)
  local copies, waits for them, and re-layouts  29.9 us (6%)
  matrix products  21.1 us (4%)
  between operations  14.8 us (3%)
  other arithmetic  7.27 us (2%)
    unnamed x4, waiting for transfers between devices  159 us
    all_gather x2, blocking collectives, body(): surface = lax.all_gather(ocean, 'member', axis=2, tiled=True)  102 us
    ppermute x14, starting transfers between devices, with_halo(): lax.ppermute(lax.slice_in_dim(block, 0, width, axis=dim), axis, backward)  62.5 us
    ppermute x14, waiting for transfers between devices, with_halo(): lax.ppermute(lax.slice_in_dim(block, block.shape[dim] - width, None, axis...  41.4 us
    ppermute x14, starting transfers between devices, with_halo(): lax.ppermute(lax.slice_in_dim(block, block.shape[dim] - width, None, axis...  31 us
    dot_general x6, matrix products, atmos_step(): jnp.einsum('kl,fmlrn->fmkrn', level_mix, advected, precision=lax.Precisio...  20.9 us
  transfers between devices with their start and end apart: 30, of which 13 were waited for; matrix products, arithmetic and copies ran while one was open for 12% of the time, Pallas kernels for 0%

commit v1 on v0

--- a/solution.py
+++ b/solution.py
@@ -86,7 +86,8 @@
     ocean_rate = jnp.stack([jnp.full_like(viscosity, OCEAN_DIFFUSION), viscosity])
     atmos_state = atmosphere
     for coupling in range(COUPLE):
-        surface = lax.all_gather(ocean, "member", axis=2, tiled=True)
+        sent = jnp.stack([ocean] * lax.axis_size("member"))
+        surface = jnp.concatenate(lax.all_to_all(sent, "member", 0, 0), axis=2)
         atmos_state = atmos_window(atmos_state, surface, diffusivity, exchange, level_mix)
         flux_terms = jnp.sum(
             exchange[:, :, None, None] * (atmos_state[:, :, 0] - surface[:, None]), axis=1

time: 474 us -> 397 us (0.84)
  blocking collectives: 102 us -> 0 us
  starting transfers between devices: 93.5 us -> 112 us
  waiting for transfers between devices: 204 us -> 209 us
    all_gather x2 -> x0, blocking collectives: 102 us -> none  [body(): surface = lax.all_gather(ocean, 'member', axis=2, tiled=True)]
    all_to_all x0 -> x2, starting transfers between devices: none -> 16.9 us  [body(): surface = jnp.concatenate(lax.all_to_all(sent, 'member', 0, 0), axis=2)]
    unnamed x4, waiting for transfers between devices: 159 us -> 163 us
    unnamed x45 -> x58, local copies, waits for them, and re-layouts: 9.13 us -> 10.5 us
  transfers between devices with their start and end apart: 30 -> 32, of which waited for: 13 -> 13; matrix products, arithmetic and copies ran while one was open for 12% -> 14% of each run, Pallas kernels for 0% -> 0%
where the time goes in v1:
time: 397 us; the launch traced here: 396 us
  waiting for transfers between devices  209 us (53%)
  starting transfers between devices  112 us (28%)
  local copies, waits for them, and re-layouts  32.3 us (8%)
  matrix products  20.7 us (5%)
  between operations  14.9 us (4%)
  other arithmetic  7.05 us (2%)
    unnamed x4, waiting for transfers between devices  163 us
    ppermute x14, starting transfers between devices, with_halo(): lax.ppermute(lax.slice_in_dim(block, 0, width, axis=dim), axis, backward)  66.2 us
    ppermute x14, waiting for transfers between devices, with_halo(): lax.ppermute(lax.slice_in_dim(block, block.shape[dim] - width, None, axis...  41.2 us
    ppermute x14, starting transfers between devices, with_halo(): lax.ppermute(lax.slice_in_dim(block, block.shape[dim] - width, None, axis...  28.5 us
    dot_general x6, matrix products, atmos_step(): jnp.einsum('kl,fmlrn->fmkrn', level_mix, advected, precision=lax.Precisio...  20.5 us
    all_to_all x2, starting transfers between devices, body(): surface = jnp.concatenate(lax.all_to_all(sent, 'member', 0, 0), axis=2)  16.9 us
    unnamed x58, local copies, waits for them, and re-layouts  10.5 us
    slice x12, local copies, waits for them, and re-layouts, atmos_step(): eastern = jnp.roll(centre, -1, axis=4)  8.78 us
  transfers between devices with their start and end apart: 32, of which 13 were waited for; matrix products, arithmetic and copies ran while one was open for 14% of the time, Pallas kernels for 0%

profile of v1, /device:TPU:48, one launch (start us, length us, event | category | flops | bytes accessed | tf_op | source)
XLA Modules:
  0.0 395.7 jit_solution(9996873179359695686)
XLA Ops:
  8.2 11.2 %collective-permute-start = (f32[2,2,8,1,1536]{4,2,3,1,0:T(8,128)S(1)}, f32[2,2,8,1,1536]{4,2,3,1,0:T(8,128)S(1)}, u32[]{:S(2)}, u32[]{:S(2)}) collective-permute-start(f32[2,2,8,1,1536]{4,2,3,1,0:T(8,128)S(1)} %get-tuple-element.118), channel_id=1, source_target_pairs={{1,0},{2,1},{3,2},{4,3},{5,4},{6,5},{7,6},{8,7},{9,8},{10,9},{11,1... | collective-permute-start | bytes 589832 | tf_op jit(solution)/shard_map/ppermute | solution.py:24
  19.4 1.9 collective-permute-start.1
  22.7 9.7 %all-to-all-start = ((f32[8,2,6,192]{3,1,2,0:T(2,128)}), f32[8,2,6,192]{3,1,2,0:T(2,128)S(1)}, u32[]{:S(2)}, u32[]{:S(2)}) async-start(f32[8,2,6,192]{3,1,2,0:T(2,128)} %stack.8), calls=%async_computation | async-start | bytes 196608 | tf_op jit(solution)/shard_map/all_to_all | solution.py:90
  33.8 4.6 %collective-permute-start.10 = (f32[2,6,1]{2,1,0:T(8,128)}, f32[2,6,1]{2,1,0:T(8,128)}, u32[]{:S(2)}, u32[]{:S(2)}) collective-permute-start(f32[2,6,1]{2,1,0:T(8,128)} %get-tuple-element.132), channel_id=1, source_target_pairs={{64,0},{128,64},{192,128},{256,192},{320,256},{384,320},{448,384},... | collective-permute-start | bytes 152 | tf_op jit(solution)/shard_map/ppermute | solution.py:24
  38.3 1.9 collective-permute-start.11
  41.6 5.0 %collective-permute-start.8 = (f32[2,1,192]{2,1,0:T(1,128)}, f32[2,1,192]{2,1,0:T(1,128)}, u32[]{:S(2)}, u32[]{:S(2)}) collective-permute-start(f32[2,1,192]{2,1,0:T(1,128)} %copy.72), channel_id=1, source_target_pairs={{1,0},{2,1},{3,2},{4,3},{5,4},{6,5},{7,6},{8,7},{9,8},{10,9},{11,1... | collective-permute-start | bytes 4616 | tf_op jit(solution)/shard_map/ppermute | solution.py:24
  46.6 3.5 fusion.206
  54.2 5.3 %fusion.5 = f32[2,2,8,6,1536]{4,2,3,1,0:T(8,128)S(1)} fusion(f32[2,2,8,6,1536]{4,2,3,1,0:T(8,128)S(1)} %copy-done.1, f32[2,2,8,1,1536]{4,2,3,1,0:T(8,128)} %copy-done.17, f32[2,2,8,1,1536]{4,2,3,1,0:T(8,128)} %copy-done.16, f32[2,2,8,6,1535]{4,2,3,1,0:T(8,128)} %get-tuple-element.115, f32[2,2,8,6,1]{4,2,3,1,0:T(8,128)} %get-tuple-element.117, ...), kind=kOutput, calls=%fused_computation.11 | convolution fusion | flops 37453824 | bytes 5701896 | tf_op jit(solution)/shard_map/kl,fmlrn->fmkrn/dot_general | solution.py:52
  61.2 1.9 collective-permute-start.2
  63.2 2.4 collective-permute-start.3
  66.3 5.9 %collective-permute-done.3 = f32[2,2,8,1,1536]{4,2,3,1,0:T(8,128)S(1)} collective-permute-done((f32[2,2,8,1,1536]{4,2,3,1,0:T(8,128)S(1)}, f32[2,2,8,1,1536]{4,2,3,1,0:T(8,128)S(1)}, u32[]{:S(2)}, u32[]{:S(2)}) %collective-permute-start.3) | collective-permute-done | bytes 196640 | tf_op jit(solution)/shard_map/ppermute | solution.py:21
  72.3 2.6 fusion.4
  76.6 1.9 collective-permute-start.4
  78.6 2.4 collective-permute-start.5
  81.7 1.9 collective-permute-start.9
  83.6 4.0 %collective-permute-done.5 = f32[2,2,8,1,1536]{4,2,3,1,0:T(8,128)S(1)} collective-permute-done((f32[2,2,8,1,1536]{4,2,3,1,0:T(8,128)S(1)}, f32[2,2,8,1,1536]{4,2,3,1,0:T(8,128)S(1)}, u32[]{:S(2)}, u32[]{:S(2)}) %collective-permute-start.5) | collective-permute-done | bytes 196640 | tf_op jit(solution)/shard_map/ppermute | solution.py:21
  87.7 2.6 fusion.3
  91.5 1.8 fusion.197
  95.4 1.8 reshape.267
  97.9 1.9 collective-permute-start.6
  99.9 85.8 %reduce-scatter.7.cloned.1.call-done = f32[192,12]{1,0:T(8,128)} async-done(((f32[1536,12]{1,0:T(8,128)}), f32[192,12]{1,0:T(8,128)}) %reduce-scatter.7.cloned.1.call-update) | async-done | bytes 9232
  186.8 1.9 collective-permute-start.7
  189.6 5.8 %collective-permute-start.12 = (f32[2,1,192]{2,1,0:T(1,128)S(1)}, f32[2,1,192]{2,1,0:T(1,128)S(1)}, u32[]{:S(2)}, u32[]{:S(2)}) collective-permute-start(f32[2,1,192]{2,1,0:T(1,128)S(1)} %get-tuple-element.128), channel_id=1, source_target_pairs={{1,0},{2,1},{3,2},{4,3},{5,4},{6,5},{7,6},{8,7},{9,8},{10,9},{11,1... | collective-permute-start | bytes 4616 | tf_op jit(solution)/shard_map/ppermute | solution.py:24
  195.4 1.9 collective-permute-start.13
  197.4 6.6 %collective-permute-start.14 = (f32[2,6,1]{2,1,0:T(8,128)S(1)}, f32[2,6,1]{2,1,0:T(8,128)S(1)}, u32[]{:S(2)}, u32[]{:S(2)}) collective-permute-start(f32[2,6,1]{2,1,0:T(8,128)S(1)} %get-tuple-element.130), channel_id=1, source_target_pairs={{64,0},{128,64},{192,128},{256,192},{320,256},{384,320},{448,384},... | collective-permute-start | bytes 152 | tf_op jit(solution)/shard_map/ppermute | solution.py:24
  205.3 2.1 collective-permute-start.15
  207.4 9.7 %collective-permute-done.15 = f32[2,6,1]{2,1,0:T(8,128)S(1)} collective-permute-done((f32[2,6,1]{2,1,0:T(8,128)S(1)}, f32[2,6,1]{2,1,0:T(8,128)S(1)}, u32[]{:S(2)}, u32[]{:S(2)}) %collective-permute-start.15) | collective-permute-done | bytes 80 | tf_op jit(solution)/shard_map/ppermute | solution.py:21
  217.9 7.2 %all-to-all-start.1 = ((f32[8,2,6,192]{3,1,2,0:T(2,128)}), f32[8,2,6,192]{3,1,2,0:T(2,128)}, u32[]{:S(2)}, u32[]{:S(2)}) async-start(f32[8,2,6,192]{3,1,2,0:T(2,128)} %stack.11), calls=%async_computation.1 | async-start | bytes 196608 | tf_op jit(solution)/shard_map/all_to_all | solution.py:90
  225.7 3.6 collective-permute-start.20
  229.3 1.9 collective-permute-start.21
  232.0 4.9 %fusion.2 = f32[2,2,8,6,1536]{4,2,3,1,0:T(8,128)S(1)} fusion(f32[2,2,8,6,1536]{4,2,3,1,0:T(8,128)S(1)} %scatter.24, f32[2,2,8,1,1536]{4,2,3,1,0:T(8,128)} %copy-done.15, f32[2,2,8,1,1536]{4,2,3,1,0:T(8,128)} %copy-done.14, f32[2,2,8,6,1535]{4,2,3,1,0:T(8,128)} %get-tuple-element.97, f32[2,2,8,6,1]{4,2,3,1,0:T(8,128)} %get-tuple-element.99, ...), kind=kOutput, calls=%fused_computation.5 | convolution fusion | flops 37453824 | bytes 5701896 | tf_op jit(solution)/shard_map/kl,fmlrn->fmkrn/dot_general | solution.py:52
  239.7 5.8 %collective-permute-start.16 = (f32[2,2,8,1,1536]{4,2,3,1,0:T(8,128)S(1)}, f32[2,2,8,1,1536]{4,2,3,1,0:T(8,128)S(1)}, u32[]{:S(2)}, u32[]{:S(2)}) collective-permute-start(f32[2,2,8,1,1536]{4,2,3,1,0:T(8,128)S(1)} %get-tuple-element.92), channel_id=1, source_target_pairs={{1,0},{2,1},{3,2},{4,3},{5,4},{6,5},{7,6},{8,7},{9,8},{10,9},{11,1... | collective-permute-start | bytes 589832 | tf_op jit(solution)/shard_map/ppermute | solution.py:24
  245.4 1.9 collective-permute-start.17
  248.6 5.9 %collective-permute-done.17 = f32[2,2,8,1,1536]{4,2,3,1,0:T(8,128)S(1)} collective-permute-done((f32[2,2,8,1,1536]{4,2,3,1,0:T(8,128)S(1)}, f32[2,2,8,1,1536]{4,2,3,1,0:T(8,128)S(1)}, u32[]{:S(2)}, u32[]{:S(2)}) %collective-permute-start.17) | collective-permute-done | bytes 196640 | tf_op jit(solution)/shard_map/ppermute | solution.py:21
  254.5 2.6 fusion.1
  258.9 1.9 collective-permute-start.18
  260.8 2.4 collective-permute-start.19
  264.0 5.9 %collective-permute-done.19 = f32[2,2,8,1,1536]{4,2,3,1,0:T(8,128)S(1)} collective-permute-done((f32[2,2,8,1,1536]{4,2,3,1,0:T(8,128)S(1)}, f32[2,2,8,1,1536]{4,2,3,1,0:T(8,128)S(1)}, u32[]{:S(2)}, u32[]{:S(2)}) %collective-permute-start.19) | collective-permute-done | bytes 196640 | tf_op jit(solution)/shard_map/ppermute | solution.py:21
  269.9 2.6 fusion
  274.1 1.8 reshape.269
  276.0 4.6 %collective-permute-start.22 = (f32[2,6,1]{2,1,0:T(8,128)S(1)}, f32[2,6,1]{2,1,0:T(8,128)S(1)}, u32[]{:S(2)}, u32[]{:S(2)}) collective-permute-start(f32[2,6,1]{2,1,0:T(8,128)S(1)} %get-tuple-element.126), channel_id=1, source_target_pairs={{64,0},{128,64},{192,128},{256,192},{320,256},{384,320},{448,384},... | collective-permute-start | bytes 152 | tf_op jit(solution)/shard_map/ppermute | solution.py:24
  280.5 1.9 collective-permute-start.23
  283.4 77.7 %reduce-scatter.9.cloned.1.call-done = f32[192,12]{1,0:T(8,128)} async-done(((f32[1536,12]{1,0:T(8,128)}), f32[192,12]{1,0:T(8,128)}) %reduce-scatter.9.cloned.1.call-update) | async-done | bytes 9232
  363.1 3.5 collective-permute-start.24
  366.6 1.9 collective-permute-start.25
  368.6 8.0 %collective-permute-start.26 = (f32[2,6,1]{2,1,0:T(8,128)S(1)}, f32[2,6,1]{2,1,0:T(8,128)S(1)}, u32[]{:S(2)}, u32[]{:S(2)}) collective-permute-start(f32[2,6,1]{2,1,0:T(8,128)S(1)} %get-tuple-element.122), channel_id=1, source_target_pairs={{64,0},{128,64},{192,128},{256,192},{320,256},{384,320},{448,384},... | collective-permute-start | bytes 152 | tf_op jit(solution)/shard_map/ppermute | solution.py:24
  376.6 1.9 collective-permute-start.27
  378.5 9.6 %collective-permute-done.27 = f32[2,6,1]{2,1,0:T(8,128)S(1)} collective-permute-done((f32[2,6,1]{2,1,0:T(8,128)S(1)}, f32[2,6,1]{2,1,0:T(8,128)S(1)}, u32[]{:S(2)}, u32[]{:S(2)}) %collective-permute-start.27) | collective-permute-done | bytes 80 | tf_op jit(solution)/shard_map/ppermute | solution.py:21
  (146 shorter events, 35.2 us)
Async XLA Ops:
  7.2 47.0 %copy-start = (f32[8,8]{1,0:T(8,128)S(1)}, f32[8,8]{1,0:T(8,128)}, u32[]{:S(2)}) copy-start(f32[8,8]{1,0:T(8,128)} %param.25) | copy-start | bytes 772
  8.2 45.2 %collective-permute-start = (f32[2,2,8,1,1536]{4,2,3,1,0:T(8,128)S(1)}, f32[2,2,8,1,1536]{4,2,3,1,0:T(8,128)S(1)}, u32[]{:S(2)}, u32[]{:S(2)}) collective-permute-start(f32[2,2,8,1,1536]{4,2,3,1,0:T(8,128)S(1)} %get-tuple-element.118), channel_id=1, source_target_pairs={{1,0},{2,1},{3,2},{4,3},{5,4},{6,5},{7,6},{8,7},{9,8},{10,9},{11,1... | collective-permute-start | bytes 589832 | tf_op jit(solution)/shard_map/ppermute | solution.py:24
  19.4 34.0 %collective-permute-start.1 = (f32[2,2,8,1,1536]{4,2,3,1,0:T(8,128)S(1)}, f32[2,2,8,1,1536]{4,2,3,1,0:T(8,128)S(1)}, u32[]{:S(2)}, u32[]{:S(2)}) collective-permute-start(f32[2,2,8,1,1536]{4,2,3,1,0:T(8,128)S(1)} %get-tuple-element.119), channel_id=1, source_target_pairs={{0,1},{1,2},{2,3},{3,4},{4,5},{5,6},{6,7},{7,8},{8,9},{9,10},{10,1... | collective-permute-start | bytes 589832 | tf_op jit(solution)/shard_map/ppermute | solution.py:21
  22.7 30.6 %all-to-all-start = ((f32[8,2,6,192]{3,1,2,0:T(2,128)}), f32[8,2,6,192]{3,1,2,0:T(2,128)S(1)}, u32[]{:S(2)}, u32[]{:S(2)}) async-start(f32[8,2,6,192]{3,1,2,0:T(2,128)} %stack.8), calls=%async_computation | async-start | bytes 196608 | tf_op jit(solution)/shard_map/all_to_all | solution.py:90
  32.4 153.3 %reduce-scatter.7.cloned.1.call-start = ((), (), s32[]{:S(2)}) async-start(), calls=%async_computation.4 | async-start | bytes 884736
  33.1 17.0 %copy-start.8 = (f32[2,6,192]{2,1,0:T(8,128)}, f32[2,6,192]{2,1,0:T(8,128)S(1)}, u32[]{:S(2)}) copy-start(f32[2,6,192]{2,1,0:T(8,128)S(1)} %copy.81) | copy-start | bytes 27652
  33.8 153.1 %collective-permute-start.10 = (f32[2,6,1]{2,1,0:T(8,128)}, f32[2,6,1]{2,1,0:T(8,128)}, u32[]{:S(2)}, u32[]{:S(2)}) collective-permute-start(f32[2,6,1]{2,1,0:T(8,128)} %get-tuple-element.132), channel_id=1, source_target_pairs={{64,0},{128,64},{192,128},{256,192},{320,256},{384,320},{448,384},... | collective-permute-start | bytes 152 | tf_op jit(solution)/shard_map/ppermute | solution.py:24
  38.3 150.4 %collective-permute-start.11 = (f32[2,6,1]{2,1,0:T(8,128)}, f32[2,6,1]{2,1,0:T(8,128)}, u32[]{:S(2)}, u32[]{:S(2)}) collective-permute-start(f32[2,6,1]{2,1,0:T(8,128)} %get-tuple-element.133), channel_id=1, source_target_pairs={{0,64},{64,128},{128,192},{192,256},{256,320},{320,384},{384,448},... | collective-permute-start | bytes 152 | tf_op jit(solution)/shard_map/ppermute | solution.py:21
  41.5 8.5 %copy-start.1 = (f32[2,2,8,6,1536]{4,2,3,1,0:T(8,128)S(1)}, f32[2,2,8,6,1536]{4,2,3,1,0:T(8,128)}, u32[]{:S(2)}) copy-start(f32[2,2,8,6,1536]{4,2,3,1,0:T(8,128)} %param.19) | copy-start | bytes 3538948
  41.6 147.2 %collective-permute-start.8 = (f32[2,1,192]{2,1,0:T(1,128)}, f32[2,1,192]{2,1,0:T(1,128)}, u32[]{:S(2)}, u32[]{:S(2)}) collective-permute-start(f32[2,1,192]{2,1,0:T(1,128)} %copy.72), channel_id=1, source_target_pairs={{1,0},{2,1},{3,2},{4,3},{5,4},{6,5},{7,6},{8,7},{9,8},{10,9},{11,1... | collective-permute-start | bytes 4616 | tf_op jit(solution)/shard_map/ppermute | solution.py:24
  53.4 6.1 %copy-start.2 = (f32[2,6,1536]{2,1,0:T(8,128)}, f32[2,6,1536]{2,1,0:T(8,128)S(1)}, u32[]{:S(2)}) copy-start(f32[2,6,1536]{2,1,0:T(8,128)S(1)} %reshape.271) | copy-start | bytes 221188
  61.1 11.1 %copy-start.20 = (f32[2]{0:T(128)S(1)}, f32[2]{0:T(128)}, u32[]{:S(2)}) copy-start(f32[2]{0:T(128)} %multiply_reduce_fusion) | copy-start | bytes 28
  61.2 5.1 %collective-permute-start.2 = (f32[2,2,8,1,1536]{4,2,3,1,0:T(8,128)S(1)}, f32[2,2,8,1,1536]{4,2,3,1,0:T(8,128)S(1)}, u32[]{:S(2)}, u32[]{:S(2)}) collective-permute-start(f32[2,2,8,1,1536]{4,2,3,1,0:T(8,128)S(1)} %get-tuple-element.112), channel_id=1, source_target_pairs={{1,0},{2,1},{3,2},{4,3},{5,4},{6,5},{7,6},{8,7},{9,8},{10,9},{11,1... | collective-permute-start | bytes 589832 | tf_op jit(solution)/shard_map/ppermute | solution.py:24
  63.2 9.1 %collective-permute-start.3 = (f32[2,2,8,1,1536]{4,2,3,1,0:T(8,128)S(1)}, f32[2,2,8,1,1536]{4,2,3,1,0:T(8,128)S(1)}, u32[]{:S(2)}, u32[]{:S(2)}) collective-permute-start(f32[2,2,8,1,1536]{4,2,3,1,0:T(8,128)S(1)} %get-tuple-element.113), channel_id=1, source_target_pairs={{0,1},{1,2},{2,3},{3,4},{4,5},{5,6},{6,7},{7,8},{8,9},{9,10},{10,1... | collective-permute-start | bytes 589832 | tf_op jit(solution)/shard_map/ppermute | solution.py:21
  72.3 2.6 copy-start.3
  76.5 5.2 %copy-start.13 = (f32[2,1,192]{2,1,0:T(1,128)S(1)}, f32[2,1,192]{2,1,0:T(1,128)}, u32[]{:S(2)}) copy-start(f32[2,1,192]{2,1,0:T(1,128)} %copy.74) | copy-start | bytes 4612
  76.5 11.1 %copy-start.21 = (f32[2]{0:T(128)S(1)}, f32[2]{0:T(128)}, u32[]{:S(2)}) copy-start(f32[2]{0:T(128)} %multiply_reduce_fusion) | copy-start | bytes 28
  76.6 5.1 %collective-permute-start.4 = (f32[2,2,8,1,1536]{4,2,3,1,0:T(8,128)S(1)}, f32[2,2,8,1,1536]{4,2,3,1,0:T(8,128)S(1)}, u32[]{:S(2)}, u32[]{:S(2)}) collective-permute-start(f32[2,2,8,1,1536]{4,2,3,1,0:T(8,128)S(1)} %get-tuple-element.106), channel_id=1, source_target_pairs={{1,0},{2,1},{3,2},{4,3},{5,4},{6,5},{7,6},{8,7},{9,8},{10,9},{11,1... | collective-permute-start | bytes 589832 | tf_op jit(solution)/shard_map/ppermute | solution.py:24
  78.6 9.1 %collective-permute-start.5 = (f32[2,2,8,1,1536]{4,2,3,1,0:T(8,128)S(1)}, f32[2,2,8,1,1536]{4,2,3,1,0:T(8,128)S(1)}, u32[]{:S(2)}, u32[]{:S(2)}) collective-permute-start(f32[2,2,8,1,1536]{4,2,3,1,0:T(8,128)S(1)} %get-tuple-element.107), channel_id=1, source_target_pairs={{0,1},{1,2},{2,3},{3,4},{4,5},{5,6},{6,7},{7,8},{8,9},{9,10},{10,1... | collective-permute-start | bytes 589832 | tf_op jit(solution)/shard_map/ppermute | solution.py:21
  81.7 107.1 %collective-permute-start.9 = (f32[2,1,192]{2,1,0:T(1,128)S(1)}, f32[2,1,192]{2,1,0:T(1,128)S(1)}, u32[]{:S(2)}, u32[]{:S(2)}) collective-permute-start(f32[2,1,192]{2,1,0:T(1,128)S(1)} %copy-done.13), channel_id=1, source_target_pairs={{0,1},{1,2},{2,3},{3,4},{4,5},{5,6},{6,7},{7,8},{8,9},{9,10},{10,1... | collective-permute-start | bytes 4616 | tf_op jit(solution)/shard_map/ppermute | solution.py:21
  97.2 91.6 %copy-start.9 = (f32[2,6,192]{2,1,0:T(8,128)S(1)}, f32[2,6,192]{2,1,0:T(8,128)}, u32[]{:S(2)}) copy-start(f32[2,6,192]{2,1,0:T(8,128)} %copy-done.8) | copy-start | bytes 27652
  97.2 91.6 %copy-start.10 = (f32[6,192]{1,0:T(8,128)S(1)}, f32[6,192]{1,0:T(8,128)}, u32[]{:S(2)}) copy-start(f32[6,192]{1,0:T(8,128)} %param.21) | copy-start | bytes 13828
  97.2 134.8 %copy-start.5 = (f32[2,2,8,6,1535]{4,2,3,1,0:T(8,128)S(1)}, f32[2,2,8,6,1535]{4,2,3,1,0:T(8,128)}, u32[]{:S(2)}) copy-start(f32[2,2,8,6,1535]{4,2,3,1,0:T(8,128)} %get-tuple-element.96) | copy-start | bytes 3536644
  97.9 133.3 %collective-permute-start.6 = (f32[2,2,8,1,1536]{4,2,3,1,0:T(8,128)S(1)}, f32[2,2,8,1,1536]{4,2,3,1,0:T(8,128)S(1)}, u32[]{:S(2)}, u32[]{:S(2)}) collective-permute-start(f32[2,2,8,1,1536]{4,2,3,1,0:T(8,128)S(1)} %get-tuple-element.100), channel_id=1, source_target_pairs={{1,0},{2,1},{3,2},{4,3},{5,4},{6,5},{7,6},{8,7},{9,8},{10,9},{11,1... | collective-permute-start | bytes 589832 | tf_op jit(solution)/shard_map/ppermute | solution.py:24
  186.8 44.5 %collective-permute-start.7 = (f32[2,2,8,1,1536]{4,2,3,1,0:T(8,128)S(1)}, f32[2,2,8,1,1536]{4,2,3,1,0:T(8,128)S(1)}, u32[]{:S(2)}, u32[]{:S(2)}) collective-permute-start(f32[2,2,8,1,1536]{4,2,3,1,0:T(8,128)S(1)} %get-tuple-element.101), channel_id=1, source_target_pairs={{0,1},{1,2},{2,3},{3,4},{4,5},{5,6},{6,7},{7,8},{8,9},{9,10},{10,1... | collective-permute-start | bytes 589832 | tf_op jit(solution)/shard_map/ppermute | solution.py:21
  189.6 27.5 %collective-permute-start.12 = (f32[2,1,192]{2,1,0:T(1,128)S(1)}, f32[2,1,192]{2,1,0:T(1,128)S(1)}, u32[]{:S(2)}, u32[]{:S(2)}) collective-permute-start(f32[2,1,192]{2,1,0:T(1,128)S(1)} %get-tuple-element.128), channel_id=1, source_target_pairs={{1,0},{2,1},{3,2},{4,3},{5,4},{6,5},{7,6},{8,7},{9,8},{10,9},{11,1... | collective-permute-start | bytes 4616 | tf_op jit(solution)/shard_map/ppermute | solution.py:24
  195.4 21.8 %collective-permute-start.13 = (f32[2,1,192]{2,1,0:T(1,128)S(1)}, f32[2,1,192]{2,1,0:T(1,128)S(1)}, u32[]{:S(2)}, u32[]{:S(2)}) collective-permute-start(f32[2,1,192]{2,1,0:T(1,128)S(1)} %get-tuple-element.129), channel_id=1, source_target_pairs={{0,1},{1,2},{2,3},{3,4},{4,5},{5,6},{6,7},{7,8},{8,9},{9,10},{10,1... | collective-permute-start | bytes 4616 | tf_op jit(solution)/shard_map/ppermute | solution.py:21
  197.4 7.9 %collective-permute-start.14 = (f32[2,6,1]{2,1,0:T(8,128)S(1)}, f32[2,6,1]{2,1,0:T(8,128)S(1)}, u32[]{:S(2)}, u32[]{:S(2)}) collective-permute-start(f32[2,6,1]{2,1,0:T(8,128)S(1)} %get-tuple-element.130), channel_id=1, source_target_pairs={{64,0},{128,64},{192,128},{256,192},{320,256},{384,320},{448,384},... | collective-permute-start | bytes 152 | tf_op jit(solution)/shard_map/ppermute | solution.py:24
  205.3 11.8 %collective-permute-start.15 = (f32[2,6,1]{2,1,0:T(8,128)S(1)}, f32[2,6,1]{2,1,0:T(8,128)S(1)}, u32[]{:S(2)}, u32[]{:S(2)}) collective-permute-start(f32[2,6,1]{2,1,0:T(8,128)S(1)} %get-tuple-element.131), channel_id=1, source_target_pairs={{0,64},{64,128},{128,192},{192,256},{256,320},{320,384},{384,448},... | collective-permute-start | bytes 152 | tf_op jit(solution)/shard_map/ppermute | solution.py:21
  217.2 14.1 %copy-start.6 = (f32[2,6,192]{2,1,0:T(8,128)}, f32[2,6,192]{2,1,0:T(8,128)S(1)}, u32[]{:S(2)}) copy-start(f32[2,6,192]{2,1,0:T(8,128)S(1)} %fusion.138) | copy-start | bytes 27652
  217.9 19.0 %all-to-all-start.1 = ((f32[8,2,6,192]{3,1,2,0:T(2,128)}), f32[8,2,6,192]{3,1,2,0:T(2,128)}, u32[]{:S(2)}, u32[]{:S(2)}) async-start(f32[8,2,6,192]{3,1,2,0:T(2,128)} %stack.11), calls=%async_computation.1 | async-start | bytes 196608 | tf_op jit(solution)/shard_map/all_to_all | solution.py:90
  225.1 135.9 %reduce-scatter.9.cloned.1.call-start = ((), (), s32[]{:S(2)}) async-start(), calls=%async_computation.5 | async-start | bytes 884736
  225.7 136.5 %collective-permute-start.20 = (f32[2,1,192]{2,1,0:T(1,128)}, f32[2,1,192]{2,1,0:T(1,128)}, u32[]{:S(2)}, u32[]{:S(2)}) collective-permute-start(f32[2,1,192]{2,1,0:T(1,128)} %get-tuple-element.124), channel_id=1, source_target_pairs={{1,0},{2,1},{3,2},{4,3},{5,4},{6,5},{7,6},{8,7},{9,8},{10,9},{11,1... | collective-permute-start | bytes 4616 | tf_op jit(solution)/shard_map/ppermute | solution.py:24
  229.3 132.9 %collective-permute-start.21 = (f32[2,1,192]{2,1,0:T(1,128)}, f32[2,1,192]{2,1,0:T(1,128)}, u32[]{:S(2)}, u32[]{:S(2)}) collective-permute-start(f32[2,1,192]{2,1,0:T(1,128)} %get-tuple-element.125), channel_id=1, source_target_pairs={{0,1},{1,2},{2,3},{3,4},{4,5},{5,6},{6,7},{7,8},{8,9},{9,10},{10,1... | collective-permute-start | bytes 4616 | tf_op jit(solution)/shard_map/ppermute | solution.py:21
  239.5 15.0 %copy-start.22 = (f32[2]{0:T(128)S(1)}, f32[2]{0:T(128)}, u32[]{:S(2)}) copy-start(f32[2]{0:T(128)} %multiply_reduce_fusion) | copy-start | bytes 28
  239.7 8.9 %collective-permute-start.16 = (f32[2,2,8,1,1536]{4,2,3,1,0:T(8,128)S(1)}, f32[2,2,8,1,1536]{4,2,3,1,0:T(8,128)S(1)}, u32[]{:S(2)}, u32[]{:S(2)}) collective-permute-start(f32[2,2,8,1,1536]{4,2,3,1,0:T(8,128)S(1)} %get-tuple-element.92), channel_id=1, source_target_pairs={{1,0},{2,1},{3,2},{4,3},{5,4},{6,5},{7,6},{8,7},{9,8},{10,9},{11,1... | collective-permute-start | bytes 589832 | tf_op jit(solution)/shard_map/ppermute | solution.py:24
  245.4 9.1 %collective-permute-start.17 = (f32[2,2,8,1,1536]{4,2,3,1,0:T(8,128)S(1)}, f32[2,2,8,1,1536]{4,2,3,1,0:T(8,128)S(1)}, u32[]{:S(2)}, u32[]{:S(2)}) collective-permute-start(f32[2,2,8,1,1536]{4,2,3,1,0:T(8,128)S(1)} %get-tuple-element.93), channel_id=1, source_target_pairs={{0,1},{1,2},{2,3},{3,4},{4,5},{5,6},{6,7},{7,8},{8,9},{9,10},{10,1... | collective-permute-start | bytes 589832 | tf_op jit(solution)/shard_map/ppermute | solution.py:21
  258.8 11.1 %copy-start.23 = (f32[2]{0:T(128)S(1)}, f32[2]{0:T(128)}, u32[]{:S(2)}) copy-start(f32[2]{0:T(128)} %multiply_reduce_fusion) | copy-start | bytes 28
  258.9 5.1 %collective-permute-start.18 = (f32[2,2,8,1,1536]{4,2,3,1,0:T(8,128)S(1)}, f32[2,2,8,1,1536]{4,2,3,1,0:T(8,128)S(1)}, u32[]{:S(2)}, u32[]{:S(2)}) collective-permute-start(f32[2,2,8,1,1536]{4,2,3,1,0:T(8,128)S(1)} %get-tuple-element.86), channel_id=1, source_target_pairs={{1,0},{2,1},{3,2},{4,3},{5,4},{6,5},{7,6},{8,7},{9,8},{10,9},{11,1... | collective-permute-start | bytes 589832 | tf_op jit(solution)/shard_map/ppermute | solution.py:24
  260.8 9.1 %collective-permute-start.19 = (f32[2,2,8,1,1536]{4,2,3,1,0:T(8,128)S(1)}, f32[2,2,8,1,1536]{4,2,3,1,0:T(8,128)S(1)}, u32[]{:S(2)}, u32[]{:S(2)}) collective-permute-start(f32[2,2,8,1,1536]{4,2,3,1,0:T(8,128)S(1)} %get-tuple-element.87), channel_id=1, source_target_pairs={{0,1},{1,2},{2,3},{3,4},{4,5},{5,6},{6,7},{7,8},{8,9},{9,10},{10,1... | collective-permute-start | bytes 589832 | tf_op jit(solution)/shard_map/ppermute | solution.py:21
  275.9 86.4 %copy-start.11 = (f32[6,192]{1,0:T(8,128)S(1)}, f32[6,192]{1,0:T(8,128)}, u32[]{:S(2)}) copy-start(f32[6,192]{1,0:T(8,128)} %param.21) | copy-start | bytes 13828
  276.0 86.3 %collective-permute-start.22 = (f32[2,6,1]{2,1,0:T(8,128)S(1)}, f32[2,6,1]{2,1,0:T(8,128)S(1)}, u32[]{:S(2)}, u32[]{:S(2)}) collective-permute-start(f32[2,6,1]{2,1,0:T(8,128)S(1)} %get-tuple-element.126), channel_id=1, source_target_pairs={{64,0},{128,64},{192,128},{256,192},{320,256},{384,320},{448,384},... | collective-permute-start | bytes 152 | tf_op jit(solution)/shard_map/ppermute | solution.py:24
  280.5 81.7 %collective-permute-start.23 = (f32[2,6,1]{2,1,0:T(8,128)S(1)}, f32[2,6,1]{2,1,0:T(8,128)S(1)}, u32[]{:S(2)}, u32[]{:S(2)}) collective-permute-start(f32[2,6,1]{2,1,0:T(8,128)S(1)} %get-tuple-element.127), channel_id=1, source_target_pairs={{0,64},{64,128},{128,192},{192,256},{256,320},{320,384},{384,448},... | collective-permute-start | bytes 152 | tf_op jit(solution)/shard_map/ppermute | solution.py:21
  283.4 105.5 %copy-start.12 = (f32[2,2,8,6,1536]{4,2,3,1,0:T(8,128)}, f32[2,2,8,6,1536]{4,2,3,1,0:T(8,128)S(1)}, u32[]{:S(2)}) copy-start(f32[2,2,8,6,1536]{4,2,3,1,0:T(8,128)S(1)} %scatter.29) | copy-start | bytes 3538948
  363.1 25.1 %collective-permute-start.24 = (f32[2,1,192]{2,1,0:T(1,128)S(1)}, f32[2,1,192]{2,1,0:T(1,128)S(1)}, u32[]{:S(2)}, u32[]{:S(2)}) collective-permute-start(f32[2,1,192]{2,1,0:T(1,128)S(1)} %get-tuple-element.120), channel_id=1, source_target_pairs={{1,0},{2,1},{3,2},{4,3},{5,4},{6,5},{7,6},{8,7},{9,8},{10,9},{11,1... | collective-permute-start | bytes 4616 | tf_op jit(solution)/shard_map/ppermute | solution.py:24
  366.6 21.6 %collective-permute-start.25 = (f32[2,1,192]{2,1,0:T(1,128)S(1)}, f32[2,1,192]{2,1,0:T(1,128)S(1)}, u32[]{:S(2)}, u32[]{:S(2)}) collective-permute-start(f32[2,1,192]{2,1,0:T(1,128)S(1)} %get-tuple-element.121), channel_id=1, source_target_pairs={{0,1},{1,2},{2,3},{3,4},{4,5},{5,6},{6,7},{7,8},{8,9},{9,10},{10,1... | collective-permute-start | bytes 4616 | tf_op jit(solution)/shard_map/ppermute | solution.py:21
  368.6 9.9 %collective-permute-start.26 = (f32[2,6,1]{2,1,0:T(8,128)S(1)}, f32[2,6,1]{2,1,0:T(8,128)S(1)}, u32[]{:S(2)}, u32[]{:S(2)}) collective-permute-start(f32[2,6,1]{2,1,0:T(8,128)S(1)} %get-tuple-element.122), channel_id=1, source_target_pairs={{64,0},{128,64},{192,128},{256,192},{320,256},{384,320},{448,384},... | collective-permute-start | bytes 152 | tf_op jit(solution)/shard_map/ppermute | solution.py:24
  376.6 11.6 %collective-permute-start.27 = (f32[2,6,1]{2,1,0:T(8,128)S(1)}, f32[2,6,1]{2,1,0:T(8,128)S(1)}, u32[]{:S(2)}, u32[]{:S(2)}) collective-permute-start(f32[2,6,1]{2,1,0:T(8,128)S(1)} %get-tuple-element.123), channel_id=1, source_target_pairs={{0,64},{64,128},{128,192},{192,256},{256,320},{320,384},{384,448},... | collective-permute-start | bytes 152 | tf_op jit(solution)/shard_map/ppermute | solution.py:21
  (8 other events, 8.9 us)
Sparse Core Ops, SparseCore 0:
  97.3 88.2 reduce-scatter.6
  276.0 84.9 reduce-scatter.8
